TPU v7x, 32 devices: a whole 2x2x4 slice. The times are simulated.
32 devices in a mesh: gx: 4 (over z), yz: 8 (over y, x, core).
Axes of the slice: x: 2, y: 2, z: 4, core: 2. Of those that a mesh axis runs over, the one named last changes fastest.
Arguments:
- positions: bfloat16 [3, 8192], P(None, ('gx', 'yz')), may hold values from 0 to 1
- species: int32 [8192], P(('gx', 'yz')), may hold values from 0 to 5
- features: bfloat16 [8192, 512], P(('gx', 'yz')), may hold values from -6 to 6
- move_dest: int32 [64], P(('gx', 'yz')), may hold values from 0 to 7, as said below
- move_slot: int32 [64], P(('gx', 'yz')), may hold values from 0 to 1, as said below
- halo_list: int32 [1024], P(('gx', 'yz')), may hold values from 0 to 255
- neighbours: int32 [8192, 64], P(('gx', 'yz')), may hold values from 0 to 383, as said below
- neighbour_count: int32 [8192], P(('gx', 'yz')), may hold values from 16 to 64
- wave_index: int32 [3, 4096], replicated, may hold values from -16 to 16, as said below
- radial_in: bfloat16 [8, 64], replicated, may hold values from -2 to 2
- radial_mid: bfloat16 [2, 64, 64], replicated, may hold values from -0.75 to 0.75
- radial_out: bfloat16 [64, 512], replicated, may hold values from -0.75 to 0.75
- up_weight: bfloat16 [2, 128, 128], replicated, may hold values from -0.5 to 0.5
- prod_weight: float32 [6, 640], replicated, may hold values from -4 to 4
- out_weight: bfloat16 [2, 128, 128], replicated, may hold values from -0.5 to 0.5
- skip_weight: bfloat16 [2, 128, 128], replicated, may hold values from -0.5 to 0.5
- charge_weight: bfloat16 [128, 8], replicated, may hold values from -0.5 to 0.5
- field_weight: float32 [8, 128], replicated, may hold values from -2 to 2
- read_weight: bfloat16 [128, 16], replicated, may hold values from -0.5 to 0.5
- read_vector: float32 [16], replicated, may hold values from -1.5 to 1.5
- force_weight: float32 [128], replicated, may hold values from -0.5 to 0.5
Outputs:
- forces: float32 [3, 8192], P(None, ('gx', 'yz'))
- energies: float32 [8192], P(('gx', 'yz'))
Inputs may be any that keep to these rules, and one draw needn't show every extreme that they name: `move_dest`: the destination lies in the same gx row. Exactly 2 blocks of each device go to other devices, at most one to any one device, and each device receives exactly 2 blocks; the others stay. `move_slot`: the 2 blocks that a device holds after the move take its 2 slots once each. `neighbours`: row of the device's table: its working atoms, then the ghosts from gx - 1, gx + 1, yz - 1, yz + 1. Never the atom itself; slots from neighbour_count on are padding. `wave_index`: row 0 runs from 1 to 8, row 1 from -16 to 16, row 2 from -2 to 2.
All inputs are finite; a program needn't handle non-finite values.
Results may differ from a plain program's by a relative error of at most 0.0028.
Values may be sent and summed in bfloat16 or wider, within the bound.
A program may use at most 64 MiB of HBM per device.

v0:
```python
import math
import jax
import jax.numpy as jnp
from jax import lax
from jax.sharding import PartitionSpec as P

highest = lax.Precision.HIGHEST
two_pi = 2.0 * math.pi
cutoff_radius = 3.5
basis_sharpness = 4.0
ewald_width = 0.1
ewald_scale = 0.01
atom_step = 64
wave_step = 512


def with_halo(value, sides, width):
    for axis, dim in sides:
        count, length = (lax.axis_size(axis), value.shape[dim])
        up = [(i, (i + 1) % count) for i in range(count)]
        down = [(j, i) for i, j in up]
        last = lax.slice_in_dim(value, length - width, length, axis=dim)
        leading = lax.slice_in_dim(value, 0, width, axis=dim)
        before = lax.ppermute(last, axis, up)
        after = lax.ppermute(leading, axis, down)
        value = jnp.concatenate([before, value, after], axis=dim)
    return value


def wave_vectors(wave_index, domains_x, domains_y):
    scales = jnp.array([two_pi / domains_x, two_pi / domains_y, two_pi], jnp.float32)
    wavevectors = wave_index.astype(jnp.float32) * scales[:, None]
    squared = jnp.sum(wavevectors * wavevectors, axis=0)
    prefactor = 8.0 * math.pi * ewald_scale / (domains_x * domains_y)
    weights = prefactor * jnp.exp(-0.5 * ewald_width * ewald_width * squared) / squared
    return (wavevectors, weights)


def phase_of(absolute, wavevectors):
    return (
        absolute[0][:, None] * wavevectors[0][None, :]
        + absolute[1][:, None] * wavevectors[1][None, :]
        + absolute[2][:, None] * wavevectors[2][None, :]
    )


def structure_terms(absolute, charges, wavevectors):
    stride = math.gcd(wavevectors.shape[1], wave_step)
    block_count = wavevectors.shape[1] // stride

    def one_block(block_index):
        wave_block = lax.dynamic_slice_in_dim(wavevectors, block_index * stride, stride, 1)
        phases = phase_of(absolute, wave_block)
        real_part = jnp.einsum("ak,aq->kq", jnp.cos(phases), charges, precision=highest)
        imag_part = jnp.einsum("ak,aq->kq", jnp.sin(phases), charges, precision=highest)
        return (real_part, imag_part)

    real_part, imag_part = lax.map(one_block, jnp.arange(block_count, dtype=jnp.int32))
    latent = charges.shape[1]
    return (real_part.reshape(-1, latent), imag_part.reshape(-1, latent))


def field_terms(absolute, wavevectors, weights, total_real, total_imag):
    scaled_real = weights[:, None] * total_real
    scaled_imag = weights[:, None] * total_imag
    right_cos = jnp.concatenate(
        [scaled_real] + [-wavevectors[direction][:, None] * scaled_imag for direction in range(3)],
        axis=1,
    )
    right_sin = jnp.concatenate(
        [scaled_imag] + [wavevectors[direction][:, None] * scaled_real for direction in range(3)],
        axis=1,
    )
    stride = math.gcd(wavevectors.shape[1], wave_step)
    block_count = wavevectors.shape[1] // stride

    def accumulate(block_index, running):
        wave_block = lax.dynamic_slice_in_dim(wavevectors, block_index * stride, stride, 1)
        phases = phase_of(absolute, wave_block)
        cos_right = lax.dynamic_slice_in_dim(right_cos, block_index * stride, stride, 0)
        sin_right = lax.dynamic_slice_in_dim(right_sin, block_index * stride, stride, 0)
        running = running + jnp.dot(jnp.cos(phases), cos_right, precision=highest)
        return running + jnp.dot(jnp.sin(phases), sin_right, precision=highest)

    initial = jnp.zeros((absolute.shape[1], right_cos.shape[1]), jnp.float32)
    return lax.fori_loop(0, block_count, accumulate, initial)


def project_pair(feature, weights):
    channels = weights.shape[1]
    row_count = feature.shape[0]
    scalar = jnp.dot(feature[:, :channels], weights[0], preferred_element_type=jnp.float32)
    vector = jnp.dot(
        feature[:, channels:].reshape(row_count * 3, channels),
        weights[1],
        preferred_element_type=jnp.float32,
    )
    return jnp.concatenate([scalar, vector.reshape(row_count, 3 * channels)], axis=1)


def edge_products(
    table_pos, table_up, centre_pos, nbr_rows, nbr_live, coeffs, radial_in, radial_mid, radial_out
):
    atom_count, slot_count = nbr_rows.shape
    edge_count = atom_count * slot_count
    table_size = table_up.shape[0]
    flat_rows = nbr_rows.reshape(edge_count)
    row_onehot = (flat_rows[:, None] == jnp.arange(table_size, dtype=jnp.int32)[None, :]).astype(
        jnp.bfloat16
    )
    picked_pos = jnp.dot(row_onehot.astype(jnp.float32), table_pos.T, precision=highest)
    offset = (picked_pos.T.reshape(3, atom_count, slot_count) - centre_pos[:, :, None]).reshape(
        3, edge_count
    )
    distance = jnp.sqrt(jnp.sum(offset * offset, axis=0))
    scaled_dist = distance / cutoff_radius
    envelope = 1.0 - 28.0 * scaled_dist**6 + 48.0 * scaled_dist**7 - 21.0 * scaled_dist**8
    alive_mask = (
        (jnp.arange(slot_count, dtype=jnp.int32)[None, :] < nbr_live[:, None])
        .astype(jnp.float32)
        .reshape(edge_count)
    )
    basis_count = radial_in.shape[0]
    centres = jnp.arange(basis_count, dtype=jnp.float32) * (cutoff_radius / (basis_count - 1))
    radial_basis = jnp.exp(-basis_sharpness * (distance[:, None] - centres[None, :]) ** 2).astype(
        jnp.bfloat16
    )
    hidden = jax.nn.silu(
        jnp.dot(radial_basis, radial_in, preferred_element_type=jnp.float32)
    ).astype(jnp.bfloat16)
    hidden = jax.nn.silu(jnp.dot(hidden, radial_mid[0], preferred_element_type=jnp.float32)).astype(
        jnp.bfloat16
    )
    hidden = jax.nn.silu(jnp.dot(hidden, radial_mid[1], preferred_element_type=jnp.float32)).astype(
        jnp.bfloat16
    )
    radial = (
        jnp.dot(hidden, radial_out, preferred_element_type=jnp.float32)
        * (envelope * alive_mask)[:, None]
    ).astype(jnp.bfloat16)
    channels = radial.shape[1] // 4
    gathered = jnp.dot(row_onehot, table_up, preferred_element_type=jnp.float32)

    def column_block(source, number):
        return source[:, number * channels : (number + 1) * channels].astype(jnp.float32)

    norm_factor = 1.0 / math.sqrt(slot_count)

    def neighbour_sum(values):
        return jnp.sum(values.reshape(atom_count, slot_count, channels), axis=1) * norm_factor

    up_scalar = column_block(gathered, 0)
    up_vector = [column_block(gathered, 1 + direction) for direction in range(3)]
    along = (
        up_vector[0] * offset[0][:, None]
        + up_vector[1] * offset[1][:, None]
        + up_vector[2] * offset[2][:, None]
    )
    scalar_msg = neighbour_sum(
        column_block(radial, 0) * up_scalar + column_block(radial, 1) * along
    )
    radial_scalar = column_block(radial, 2) * up_scalar
    radial_vector = column_block(radial, 3)
    vector_msg = [
        neighbour_sum(
            radial_scalar * offset[direction][:, None] + radial_vector * up_vector[direction]
        )
        for direction in range(3)
    ]
    square_sum = (
        vector_msg[0] * vector_msg[0]
        + vector_msg[1] * vector_msg[1]
        + vector_msg[2] * vector_msg[2]
    )
    path_weights = [coeffs[:, number * channels : (number + 1) * channels] for number in range(5)]
    scalar_prod = (
        path_weights[0] * scalar_msg
        + path_weights[1] * scalar_msg * scalar_msg
        + path_weights[2] * square_sum
    )
    vector_prod = [
        path_weights[3] * vector_msg[direction]
        + path_weights[4] * scalar_msg * vector_msg[direction]
        for direction in range(3)
    ]
    return jnp.concatenate([scalar_prod] + vector_prod, axis=1).astype(jnp.bfloat16)


def atom_results(
    work_feat,
    products,
    charges,
    efield,
    out_weight,
    skip_weight,
    field_weight,
    read_weight,
    read_vector,
    force_weight,
):
    channels = out_weight.shape[1]
    latent = charges.shape[1]
    mixed_feat = project_pair(products, out_weight) + project_pair(work_feat, skip_weight)
    potential = efield[:, :latent]
    scalars = mixed_feat[:, :channels] + jnp.dot(potential, field_weight, precision=highest)
    readout = jax.nn.silu(
        jnp.dot(scalars.astype(jnp.bfloat16), read_weight, preferred_element_type=jnp.float32)
    )
    energy = jnp.dot(readout, read_vector, precision=highest) + 0.5 * jnp.sum(
        charges * potential, axis=1
    )
    forces = [
        jnp.dot(
            mixed_feat[:, (1 + direction) * channels : (2 + direction) * channels],
            force_weight,
            precision=highest,
        )
        + jnp.sum(charges * efield[:, (1 + direction) * latent : (2 + direction) * latent], axis=1)
        for direction in range(3)
    ]
    return jnp.stack(forces + [energy])


def pick_float(chosen, source):
    return jnp.einsum("ab,bij->aij", chosen, source, precision=highest)


def pick_half(chosen, source):
    return jnp.einsum(
        "ab,bij->aij", chosen.astype(jnp.bfloat16), source, preferred_element_type=jnp.float32
    )


def on_device(
    positions,
    species,
    features,
    move_dest,
    move_slot,
    halo_list,
    neighbours,
    neighbour_count,
    wave_index,
    radial_in,
    radial_mid,
    radial_out,
    up_weight,
    prod_weight,
    out_weight,
    skip_weight,
    charge_weight,
    field_weight,
    read_weight,
    read_vector,
    force_weight,
):
    blocks = move_dest.shape[0]
    atom_count = positions.shape[1]
    block_size = atom_count // blocks
    channels = up_weight.shape[1]
    domains_x = lax.axis_size("gx")
    domains_y = lax.axis_size("yz")
    column = lax.axis_index("yz")
    layer_row = lax.axis_index("gx")
    column_f = column.astype(jnp.float32)
    slot_iota = jnp.arange(blocks, dtype=jnp.int32)
    slot_float = slot_iota.astype(jnp.float32)
    peer_iota = jnp.arange(domains_y, dtype=jnp.int32)
    moving = move_dest != column
    meta_rows = jnp.stack(
        [
            move_slot.astype(jnp.float32) + 1.0,
            slot_float,
            jnp.zeros((blocks,), jnp.float32) + column_f + 1.0,
            move_dest.astype(jnp.float32) + 1.0,
        ],
        axis=1,
    )
    home_geo = jnp.concatenate(
        [
            positions.reshape(3, blocks, block_size).transpose(1, 0, 2),
            species.astype(jnp.bfloat16).reshape(blocks, 1, block_size),
            jnp.broadcast_to(meta_rows[:, :, None], (blocks, 4, block_size)).astype(jnp.bfloat16),
        ],
        axis=1,
    )
    home_feat = features.reshape(blocks, block_size, 4 * channels)
    stay_pick = ((move_slot[None, :] == slot_iota[:, None]) & ~moving[None, :]).astype(jnp.float32)
    send_pick = ((move_dest[None, :] == peer_iota[:, None]) & moving[None, :]).astype(jnp.float32)
    out_geo = pick_half(send_pick, home_geo).astype(jnp.bfloat16)
    out_feat = pick_half(send_pick, home_feat).astype(jnp.bfloat16)
    in_geo, in_feat = (
        lax.all_to_all(out_geo, "yz", split_axis=0, concat_axis=0, tiled=True),
        lax.all_to_all(out_feat, "yz", split_axis=0, concat_axis=0, tiled=True),
    )
    arrive_pick = (
        in_geo[:, 4, 0].astype(jnp.float32)[None, :] == slot_float[:, None] + 1.0
    ).astype(jnp.float32)
    arrive_geo = pick_half(arrive_pick, in_geo)
    arrive_feat = pick_half(arrive_pick, in_feat)
    work_geo = pick_half(stay_pick, home_geo) + arrive_geo
    work_feat = (
        (pick_half(stay_pick, home_feat) + arrive_feat)
        .astype(jnp.bfloat16)
        .reshape(atom_count, 4 * channels)
    )
    work_pos = work_geo[:, :3].transpose(1, 0, 2).reshape(3, atom_count)
    work_species = work_geo[:, 3].reshape(atom_count)
    home_of_slot = work_geo[:, 6, 0] - 1.0
    arrived = home_of_slot != column_f
    list_pick = (halo_list[:, None] == jnp.arange(atom_count, dtype=jnp.int32)[None, :]).astype(
        jnp.float32
    )
    send_pos = jnp.dot(work_pos, list_pick.T, precision=highest).astype(jnp.bfloat16)
    send_feat = jnp.dot(
        list_pick.astype(jnp.bfloat16), work_feat, preferred_element_type=jnp.float32
    ).astype(jnp.bfloat16)
    ext_pos, ext_feat = (
        with_halo(send_pos[None, None], (("gx", 0), ("yz", 1)), 1),
        with_halo(send_feat[None, None], (("gx", 0), ("yz", 1)), 1),
    )
    unit_axes = jnp.eye(3, dtype=jnp.float32)
    ghost_pos = [
        ext_pos[0, 1].astype(jnp.float32) - unit_axes[0][:, None],
        ext_pos[2, 1].astype(jnp.float32) + unit_axes[0][:, None],
        ext_pos[1, 0].astype(jnp.float32) - unit_axes[1][:, None],
        ext_pos[1, 2].astype(jnp.float32) + unit_axes[1][:, None],
    ]
    table_pos = jnp.concatenate([work_pos] + ghost_pos, axis=1)
    table_feat = jnp.concatenate(
        [work_feat, ext_feat[0, 1], ext_feat[2, 1], ext_feat[1, 0], ext_feat[1, 2]], axis=0
    )
    anchor = jnp.stack([layer_row.astype(jnp.float32), column_f, jnp.zeros((), jnp.float32)])
    absolute = work_pos + anchor[:, None]
    charges = jnp.dot(work_feat[:, :channels], charge_weight, preferred_element_type=jnp.float32)
    wavevectors, weights = wave_vectors(wave_index, domains_x, domains_y)
    part_real, part_imag = structure_terms(absolute, charges, wavevectors)
    total_real, total_imag = lax.psum((part_real, part_imag), ("gx", "yz"))
    table_up = project_pair(table_feat, up_weight).astype(jnp.bfloat16)
    onehot = (
        work_species[:, None] == jnp.arange(prod_weight.shape[0], dtype=jnp.float32)[None, :]
    ).astype(jnp.float32)
    coeffs = jnp.dot(onehot, prod_weight, precision=highest)
    block_count = atom_count // atom_step

    def edge_block(pieces):
        return edge_products(
            table_pos,
            table_up,
            pieces[2],
            pieces[0],
            pieces[1],
            pieces[3],
            radial_in,
            radial_mid,
            radial_out,
        )

    products = lax.map(
        edge_block,
        (
            neighbours.reshape(block_count, atom_step, -1),
            neighbour_count.reshape(block_count, atom_step),
            work_pos.reshape(3, block_count, atom_step).transpose(1, 0, 2),
            coeffs.reshape(block_count, atom_step, -1),
        ),
    ).reshape(atom_count, 4 * channels)
    efield = field_terms(absolute, wavevectors, weights, total_real, total_imag)
    results = atom_results(
        work_feat,
        products,
        charges,
        efield,
        out_weight,
        skip_weight,
        field_weight,
        read_weight,
        read_vector,
        force_weight,
    )
    res_blocks = results.reshape(4, blocks, block_size).transpose(1, 0, 2)
    back_pick = (
        (home_of_slot[None, :] == peer_iota.astype(jnp.float32)[:, None]) & arrived[None, :]
    ).astype(jnp.float32)
    sent_back = pick_float(back_pick, res_blocks)
    came_back = lax.all_to_all(sent_back, "yz", split_axis=0, concat_axis=0, tiled=True)
    remote_pick = ((move_dest[:, None] == peer_iota[None, :]) & moving[:, None]).astype(jnp.float32)
    remote = pick_float(remote_pick, came_back)
    home_res = pick_float(stay_pick.T, res_blocks) + remote
    flat_res = home_res.transpose(1, 0, 2).reshape(4, atom_count)
    return (flat_res[:3], flat_res[3])


def solution(mesh):
    in_specs = (
        P(None, ("gx", "yz")),
        P(("gx", "yz")),
        P(("gx", "yz"), None),
        P(("gx", "yz")),
        P(("gx", "yz")),
        P(("gx", "yz")),
        P(("gx", "yz"), None),
        P(("gx", "yz")),
        P(),
        P(),
        P(),
        P(),
        P(),
        P(),
        P(),
        P(),
        P(),
        P(),
        P(),
        P(),
        P(),
    )
    out_specs = (P(None, ("gx", "yz")), P(("gx", "yz")))
    return jax.shard_map(
        on_device, mesh=mesh, in_specs=in_specs, out_specs=out_specs, check_vma=False
    )
```

profile of v0, /device:TPU:0, one launch (start us, length us, event | category | flops | bytes accessed | tf_op | source)
XLA Modules:
  0.0 382.4 jit_solution(8578587456457187002)
XLA Ops:
  12.4 5.2 %all-to-all-start = ((bf16[8,8,128]{2,1,0:T(8,128)(2,1)}), bf16[8,8,128]{2,1,0:T(8,128)(2,1)S(1)}, u32[]{:S(2)}, u32[]{:S(2)}) async-start(bf16[8,8,128]{2,1,0:T(8,128)(2,1)} %copy.64), calls=%async_computation | async-start | bytes 32768 | tf_op jit(solution)/shard_map/all_to_all | solution.py:293
  24.0 4.2 %all-to-all-start.1 = ((bf16[8,128,512]{2,1,0:T(8,128)(2,1)}), bf16[8,128,512]{2,1,0:T(8,128)(2,1)S(1)}, u32[]{:S(2)}, u32[]{:S(2)}) async-start(bf16[8,128,512]{2,1,0:T(8,128)(2,1)} %copy.71), calls=%async_computation.1 | async-start | bytes 2097152 | tf_op jit(solution)/shard_map/all_to_all | solution.py:294
  37.3 5.7 %collective-permute-done.2 = bf16[3,1,3,32]{3,2,1,0:T(4,128)(2,1)S(1)} collective-permute-done((bf16[3,1,3,32]{3,2,1,0:T(4,128)(2,1)S(1)}, bf16[3,1,3,32]{3,2,1,0:T(4,128)(2,1)S(1)}, u32[]{:S(2)}, u32[]{:S(2)}) %collective-permute-start.2) | collective-permute-done | bytes 608 | tf_op jit(solution)/shard_map/ppermute | solution.py:24
  49.9 56.6 %while.37 = (s32[]{:T(128)}, f32[8,512,8]{1,2,0:T(8,128)}, f32[8,512,8]{1,2,0:T(8,128)}, f32[3,256]{1,0:T(4,128)S(1)}, s32[8]{0:T(128)S(1)}, /*index=5*/f32[3,40...) while((s32[]{:T(128)}, f32[8,512,8]{1,2,0:T(8,128)}, ...), condition=%wide.region_9.10_spmd, body=%wide.region_8.9_spmd.sunk | while | flops 26476552 | bytes 87259 | solution.py:58
  110.5 121.8 %all-reduce.3.cloned.1.call-done = (f32[4096,8]{0,1:T(8,128)}, f32[4096,8]{0,1:T(8,128)}) async-done(((f32[4096,8]{0,1:T(8,128)}, f32[4096,8]{0,1:T(8,128)}), (f32[4096,8]{0,1:T(8,128)}, f32[4096,8]{0,1:T(8,128)})) %all-reduce.3.cloned.1.call-update) | async-done | bytes 262160 | tf_op jit(solution)/shard_map/psum | solution.py:338
  233.5 54.9 %while.38 = (s32[]{:T(128)}, f32[256,32]{0,1:T(8,128)S(1)}, f32[3,256]{1,0:T(4,128)S(1)}, f32[3,4096]{1,0:T(4,128)S(1)}, f32[4096,32]{0,1:T(8,128)S(1)}, /*index...) while((s32[]{:T(128)}, f32[256,32]{0,1:T(8,128)S(1)}, ...), condition=%wide.region_13.14_spmd.clone, body=%wide.region_12.13_spmd.clone.sunk | while | flops 101998600 | bytes 299225 | solution.py:86
  237.2 3.1 convolution_add_fusion.9
  241.0 3.1 convolution_add_fusion.8
  244.1 3.1 convolution_add_fusion.9
  251.0 3.1 convolution_add_fusion.9
  257.8 3.1 convolution_add_fusion.9
  264.7 3.1 convolution_add_fusion.9
  268.5 3.1 convolution_add_fusion.8
  271.6 3.1 convolution_add_fusion.9
  278.4 3.1 convolution_add_fusion.9
  282.2 3.1 convolution_add_fusion.8
  285.3 3.1 convolution_add_fusion.9
  291.8 70.9 %while.36 = (s32[]{:T(128)}, bf16[4,64,512]{2,1,0:T(8,128)(2,1)S(1)}, f32[4,64,640]{2,1,0:T(8,128)S(1)}, s32[4,64,64]{2,1,0:T(8,128)S(1)}, f32[3,384]{1,0:T(4,12...) while((s32[]{:T(128)}, ...), condition=%wide.region_6.7_spmd, body=%wide.region_0.6_spmd.sunk | while | flops 2032549888 | bytes 45476804 | solution.py:359
  293.0 3.1 multiply_reduce_fusion.7
  298.7 4.6 %multiply_convert_fusion.13 = bf16[4096,512]{1,0:T(8,128)(2,1)} fusion(bf16[64,512]{1,0:T(8,128)(2,1)S(1)} %get-tuple-element.587, f32[4096]{0:T(1024)S(1)} %get-tuple-element.517, bf16[4096,64]{0,1:T(8,128)(2,1)} %multiply_convert_fusion.12, bf16[2,64,64]{2,1,0:T(8,128)(2,1)S(1)} %get-tuple-element.586), kind=kOutput, calls=%fused_computation.clone.1 | convolution fusion | flops 307494912 | bytes 4816896 | tf_op jit(solution)/shard_map/while/body/eval_jaxpr/dot_general | solution.py:138
  306.1 3.4 bitcast_reduce_fusion.5
  310.6 3.1 multiply_reduce_fusion.7
  316.3 4.6 %multiply_convert_fusion.13 = bf16[4096,512]{1,0:T(8,128)(2,1)} fusion(bf16[64,512]{1,0:T(8,128)(2,1)S(1)} %get-tuple-element.587, f32[4096]{0:T(1024)S(1)} %get-tuple-element.517, bf16[4096,64]{0,1:T(8,128)(2,1)} %multiply_convert_fusion.12, bf16[2,64,64]{2,1,0:T(8,128)(2,1)S(1)} %get-tuple-element.586), kind=kOutput, calls=%fused_computation.clone.1 | convolution fusion | flops 307494912 | bytes 4816896 | tf_op jit(solution)/shard_map/while/body/eval_jaxpr/dot_general | solution.py:138
  323.8 3.4 bitcast_reduce_fusion.5
  328.3 3.1 multiply_reduce_fusion.7
  334.0 4.6 %multiply_convert_fusion.13 = bf16[4096,512]{1,0:T(8,128)(2,1)} fusion(bf16[64,512]{1,0:T(8,128)(2,1)S(1)} %get-tuple-element.587, f32[4096]{0:T(1024)S(1)} %get-tuple-element.517, bf16[4096,64]{0,1:T(8,128)(2,1)} %multiply_convert_fusion.12, bf16[2,64,64]{2,1,0:T(8,128)(2,1)S(1)} %get-tuple-element.586), kind=kOutput, calls=%fused_computation.clone.1 | convolution fusion | flops 307494912 | bytes 4816896 | tf_op jit(solution)/shard_map/while/body/eval_jaxpr/dot_general | solution.py:138
  341.5 3.4 bitcast_reduce_fusion.5
  346.0 3.1 multiply_reduce_fusion.7
  351.7 4.6 %multiply_convert_fusion.13 = bf16[4096,512]{1,0:T(8,128)(2,1)} fusion(bf16[64,512]{1,0:T(8,128)(2,1)S(1)} %get-tuple-element.587, f32[4096]{0:T(1024)S(1)} %get-tuple-element.517, bf16[4096,64]{0,1:T(8,128)(2,1)} %multiply_convert_fusion.12, bf16[2,64,64]{2,1,0:T(8,128)(2,1)S(1)} %get-tuple-element.586), kind=kOutput, calls=%fused_computation.clone.1 | convolution fusion | flops 307494912 | bytes 4816896 | tf_op jit(solution)/shard_map/while/body/eval_jaxpr/dot_general | solution.py:138
  359.1 3.4 bitcast_reduce_fusion.5
  365.8 3.6 all-to-all-start.2
  369.6 4.5 %all-to-all-done.2 = f32[8,4,128]{2,1,0:T(4,128)S(1)} async-done(((f32[8,4,128]{2,1,0:T(4,128)}), f32[8,4,128]{2,1,0:T(4,128)S(1)}, u32[]{:S(2)}, u32[]{:S(2)}) %all-to-all-start.2) | async-done | bytes 16416 | tf_op jit(solution)/shard_map/all_to_all | solution.py:386
  (336 shorter events, 138.1 us)
Async XLA Ops:
  7.2 11.3 %copy-start = (bf16[256,512]{1,0:T(8,128)(2,1)S(1)}, bf16[256,512]{1,0:T(8,128)(2,1)}, u32[]{:S(2)}) copy-start(bf16[256,512]{1,0:T(8,128)(2,1)} %param.30) | copy-start | bytes 786436
  7.2 14.4 %copy-start.18 = (f32[3]{0:T(128)S(1)}, f32[3]{0:T(128)}, u32[]{:S(2)}) copy-start(f32[3]{0:T(128)} %constant.114.clone) | copy-start | bytes 40
  7.2 14.4 %copy-start.6 = (s32[3,4096]{1,0:T(4,128)S(1)}, s32[3,4096]{1,0:T(4,128)}, u32[]{:S(2)}) copy-start(s32[3,4096]{1,0:T(4,128)} %param.36) | copy-start | bytes 147460
  8.6 14.6 %copy-start.14 = (pred[2]{0:T(512)(128)(4,1)}, pred[2]{0:T(512)(128)(4,1)S(1)}, u32[]{:S(2)}) copy-start(pred[2]{0:T(512)(128)(4,1)S(1)} %get-tuple-element.307) | copy-start | bytes 10
  8.6 14.6 %copy-start.19 = (pred[2]{0:T(512)(128)(4,1)}, pred[2]{0:T(512)(128)(4,1)S(1)}, u32[]{:S(2)}) copy-start(pred[2]{0:T(512)(128)(4,1)S(1)} %get-tuple-element.306) | copy-start | bytes 10
  12.4 11.6 %all-to-all-start = ((bf16[8,8,128]{2,1,0:T(8,128)(2,1)}), bf16[8,8,128]{2,1,0:T(8,128)(2,1)S(1)}, u32[]{:S(2)}, u32[]{:S(2)}) async-start(bf16[8,8,128]{2,1,0:T(8,128)(2,1)} %copy.64), calls=%async_computation | async-start | bytes 32768 | tf_op jit(solution)/shard_map/all_to_all | solution.py:293
  18.5 4.7 %copy-start.2 = (s32[256,64]{0,1:T(8,128)S(1)}, s32[256,64]{0,1:T(8,128)}, u32[]{:S(2)}) copy-start(s32[256,64]{0,1:T(8,128)} %param.34) | copy-start | bytes 196612
  19.8 3.6 copy-start.16
  21.9 6.7 %copy-start.17 = (s32[32]{0:T(128)S(1)}, s32[32]{0:T(128)}, u32[]{:S(2)}) copy-start(s32[32]{0:T(128)} %param.33) | copy-start | bytes 388
  21.9 11.5 %copy-start.7 = (f32[6,640]{1,0:T(8,128)S(1)}, f32[6,640]{1,0:T(8,128)}, u32[]{:S(2)}) copy-start(f32[6,640]{1,0:T(8,128)} %param.41) | copy-start | bytes 46084
  24.0 19.8 %all-to-all-start.1 = ((bf16[8,128,512]{2,1,0:T(8,128)(2,1)}), bf16[8,128,512]{2,1,0:T(8,128)(2,1)S(1)}, u32[]{:S(2)}, u32[]{:S(2)}) async-start(bf16[8,128,512]{2,1,0:T(8,128)(2,1)} %copy.71), calls=%async_computation.1 | async-start | bytes 2097152 | tf_op jit(solution)/shard_map/all_to_all | solution.py:294
  28.2 21.6 %copy-start.23 = (bf16[128,8]{0,1:T(8,128)(2,1)S(1)}, bf16[128,8]{0,1:T(8,128)(2,1)}, u32[]{:S(2)}) copy-start(bf16[128,8]{0,1:T(8,128)(2,1)} %param.44) | copy-start | bytes 6148
  28.2 204.1 %all-reduce.3.cloned.1.call-start = ((), (), s32[]{:S(2)}) async-start(), calls=%async_computation.3 | async-start | bytes 524288 | tf_op jit(solution)/shard_map/psum | solution.py:338
  28.8 5.8 %collective-permute-start = (bf16[1,1,3,32]{3,2,1,0:T(4,128)(2,1)S(1)}, bf16[1,1,3,32]{3,2,1,0:T(4,128)(2,1)S(1)}, u32[]{:S(2)}, u32[]{:S(2)}) collective-permute-start(bf16[1,1,3,32]{3,2,1,0:T(4,128)(2,1)S(1)} %fusion.86), channel_id=1, source_target_pairs={{0,8},{8,16},{16,24},{24,0},{1,9},{9,17},{17,25},{25,1},{2,10},{10... | collective-permute-start | bytes 584 | tf_op jit(solution)/shard_map/ppermute | solution.py:24
  30.3 4.2 %collective-permute-start.1 = (bf16[1,1,3,32]{3,2,1,0:T(4,128)(2,1)S(1)}, bf16[1,1,3,32]{3,2,1,0:T(4,128)(2,1)S(1)}, u32[]{:S(2)}, u32[]{:S(2)}) collective-permute-start(bf16[1,1,3,32]{3,2,1,0:T(4,128)(2,1)S(1)} %fusion.86), channel_id=1, source_target_pairs={{8,0},{16,8},{24,16},{0,24},{9,1},{17,9},{25,17},{1,25},{10,2},{18... | collective-permute-start | bytes 584 | tf_op jit(solution)/shard_map/ppermute | solution.py:25
  32.7 13.0 %copy-start.27 = (f32[2]{0:T(128)}, f32[2]{0:T(128)S(1)}, u32[]{:S(2)}) copy-start(f32[2]{0:T(128)S(1)} %fusion.147) | copy-start | bytes 28
  34.6 8.5 %collective-permute-start.2 = (bf16[3,1,3,32]{3,2,1,0:T(4,128)(2,1)S(1)}, bf16[3,1,3,32]{3,2,1,0:T(4,128)(2,1)S(1)}, u32[]{:S(2)}, u32[]{:S(2)}) collective-permute-start(bf16[3,1,3,32]{3,2,1,0:T(4,128)(2,1)S(1)} %pad_maximum_fusion.5), channel_id=1, source_target_pairs={{0,1},{1,2},{2,3},{3,4},{4,5},{5,6},{6,7},{7,0},{8,9},{9,10},{10,1... | collective-permute-start | bytes 1736 | tf_op jit(solution)/shard_map/ppermute | solution.py:24
  34.6 8.4 %collective-permute-start.3 = (bf16[3,1,3,32]{3,2,1,0:T(4,128)(2,1)S(1)}, bf16[3,1,3,32]{3,2,1,0:T(4,128)(2,1)S(1)}, u32[]{:S(2)}, u32[]{:S(2)}) collective-permute-start(bf16[3,1,3,32]{3,2,1,0:T(4,128)(2,1)S(1)} %pad_maximum_fusion.5), channel_id=1, source_target_pairs={{1,0},{2,1},{3,2},{4,3},{5,4},{6,5},{7,6},{0,7},{9,8},{10,9},{11,1... | collective-permute-start | bytes 1736 | tf_op jit(solution)/shard_map/ppermute | solution.py:25
  45.9 61.9 %collective-permute-start.4 = (bf16[1,1,32,512]{3,2,1,0:T(8,128)(2,1)S(1)}, bf16[1,1,32,512]{3,2,1,0:T(8,128)(2,1)S(1)}, u32[]{:S(2)}, u32[]{:S(2)}) collective-permute-start(bf16[1,1,32,512]{3,2,1,0:T(8,128)(2,1)S(1)} %fusion.84), channel_id=1, source_target_pairs={{0,8},{8,16},{16,24},{24,0},{1,9},{9,17},{17,25},{25,1},{2,10},{10... | collective-permute-start | bytes 98312 | tf_op jit(solution)/shard_map/ppermute | solution.py:24
  47.5 60.3 %collective-permute-start.5 = (bf16[1,1,32,512]{3,2,1,0:T(8,128)(2,1)S(1)}, bf16[1,1,32,512]{3,2,1,0:T(8,128)(2,1)S(1)}, u32[]{:S(2)}, u32[]{:S(2)}) collective-permute-start(bf16[1,1,32,512]{3,2,1,0:T(8,128)(2,1)S(1)} %fusion.84), channel_id=1, source_target_pairs={{8,0},{16,8},{24,16},{0,24},{9,1},{17,9},{25,17},{1,25},{10,2},{18... | collective-permute-start | bytes 98312 | tf_op jit(solution)/shard_map/ppermute | solution.py:25
  49.9 57.3 %copy-start.3 = (bf16[2,128,128]{2,1,0:T(8,128)(2,1)S(1)}, bf16[2,128,128]{2,1,0:T(8,128)(2,1)}, u32[]{:S(2)}) copy-start(bf16[2,128,128]{2,1,0:T(8,128)(2,1)} %param.43) | copy-start | bytes 196612
  107.8 181.4 %collective-permute-start.6 = (bf16[3,1,32,512]{3,2,1,0:T(8,128)(2,1)S(1)}, bf16[3,1,32,512]{3,2,1,0:T(8,128)(2,1)}, u32[]{:S(2)}, u32[]{:S(2)}) collective-permute-start(bf16[3,1,32,512]{3,2,1,0:T(8,128)(2,1)S(1)} %pad_maximum_fusion.3), channel_id=1, source_target_pairs={{0,1},{1,2},{2,3},{3,4},{4,5},{5,6},{6,7},{7,0},{8,9},{9,10},{10,1... | collective-permute-start | bytes 294920 | tf_op jit(solution)/shard_map/ppermute | solution.py:24
  107.9 182.1 %collective-permute-start.7 = (bf16[3,1,32,512]{3,2,1,0:T(8,128)(2,1)S(1)}, bf16[3,1,32,512]{3,2,1,0:T(8,128)(2,1)}, u32[]{:S(2)}, u32[]{:S(2)}) collective-permute-start(bf16[3,1,32,512]{3,2,1,0:T(8,128)(2,1)S(1)} %pad_maximum_fusion.3), channel_id=1, source_target_pairs={{1,0},{2,1},{3,2},{4,3},{5,4},{6,5},{7,6},{0,7},{9,8},{10,9},{11,1... | collective-permute-start | bytes 294920 | tf_op jit(solution)/shard_map/ppermute | solution.py:25
  233.5 57.4 %copy-start.4 = (bf16[2,128,128]{2,1,0:T(8,128)(2,1)S(1)}, bf16[2,128,128]{2,1,0:T(8,128)(2,1)}, u32[]{:S(2)}) copy-start(bf16[2,128,128]{2,1,0:T(8,128)(2,1)} %param.40) | copy-start | bytes 196612
  288.4 3.3 copy-start.9
  288.4 3.3 copy-start.21
  291.7 71.1 %copy-start.5 = (bf16[2,128,128]{2,1,0:T(8,128)(2,1)S(1)}, bf16[2,128,128]{2,1,0:T(8,128)(2,1)}, u32[]{:S(2)}) copy-start(bf16[2,128,128]{2,1,0:T(8,128)(2,1)} %param.42) | copy-start | bytes 196612
  362.9 6.6 %copy-start.20 = (pred[2]{0:T(512)(128)(4,1)S(1)}, pred[2]{0:T(512)(128)(4,1)}, u32[]{:S(2)}) copy-start(pred[2]{0:T(512)(128)(4,1)} %copy-done.19) | copy-start | bytes 10
  362.9 6.6 %copy-start.26 = (s32[2]{0:T(128)S(1)}, s32[2]{0:T(128)}, u32[]{:S(2)}) copy-start(s32[2]{0:T(128)} %param.32) | copy-start | bytes 28
  363.0 11.2 %copy-start.13 = (s32[2]{0:T(128)S(1)}, s32[2]{0:T(128)}, u32[]{:S(2)}) copy-start(s32[2]{0:T(128)} %param.31) | copy-start | bytes 28
  363.0 11.1 %copy-start.15 = (pred[2]{0:T(512)(128)(4,1)S(1)}, pred[2]{0:T(512)(128)(4,1)}, u32[]{:S(2)}) copy-start(pred[2]{0:T(512)(128)(4,1)} %copy-done.14) | copy-start | bytes 10
  365.8 8.4 %all-to-all-start.2 = ((f32[8,4,128]{2,1,0:T(4,128)}), f32[8,4,128]{2,1,0:T(4,128)S(1)}, u32[]{:S(2)}, u32[]{:S(2)}) async-start(f32[8,4,128]{2,1,0:T(4,128)} %copy.79), calls=%async_computation.2 | async-start | bytes 32768 | tf_op jit(solution)/shard_map/all_to_all | solution.py:386
  (14 other events, 29.1 us)
Sparse Core Ops, SparseCore 0:
  107.9 124.3 all-reduce.2
where the time goes:
time: 384 us; the launch traced here: 382 us
  matrix products  152 us (40%)
  waiting for transfers between devices  132 us (34%)
  local copies, waits for them, and re-layouts  29 us (8%)
  starting transfers between devices  26.1 us (7%)
  other arithmetic  22 us (6%)
  between operations  14.7 us (4%)
  loops' own time  6.29 us (2%)
    psum x1, waiting for transfers between devices, on_device(): total_real, total_imag = lax.psum((part_real, part_imag), ('gx', 'yz'))  122 us
    dot_general x8, matrix products, accumulate(): return running + jnp.dot(jnp.sin(phases), sin_right, precision=highest)  24.7 us
    dot_general x8, matrix products, accumulate(): running = running + jnp.dot(jnp.cos(phases), cos_right, precision=highest)  24.5 us
    dot_general x8, matrix products, one_block(): jnp.einsum('ak,aq->kq', jnp.sin(phases), charges, precision=highest)  23.1 us
    dot_general x8, matrix products, one_block(): jnp.einsum('ak,aq->kq', jnp.cos(phases), charges, precision=highest)  22.9 us
    dot_general x4, matrix products, edge_products(): jnp.dot(hidden, radial_out, preferred_element_type=jnp.float32)  18.3 us
    reduce_sum x4, other arithmetic, neighbour_sum(): jnp.sum(values.reshape(atom_count, slot_count, channels), axis=1)  13.6 us
    dot_general x4, matrix products, edge_products(): jnp.dot(row_onehot.astype(jnp.float32), table_pos.T, precision=highest)  12.4 us
  transfers between devices with their start and end apart: 12, of which 3 were waited for; matrix products, arithmetic and copies ran while one was open for 31% of the time, Pallas kernels for 0%

commit v1 on v0

--- a/solution.py
+++ b/solution.py
@@ -1,3 +1,4 @@
+import functools
 import math
 import jax
 import jax.numpy as jnp
@@ -12,6 +13,15 @@
 ewald_scale = 0.01
 atom_step = 64
 wave_step = 512
+
+
+def review_strips_all(block_in, device_axis, which_axis):
+    for h in (device_axis, which_axis):
+        block_in = jax.lax.psum(block_in, h)
+    return block_in
+
+
+treat_cells = functools.partial(review_strips_all, device_axis="yz", which_axis="gx")
 
 
 def with_halo(value, sides, width):
@@ -335,7 +345,7 @@
     charges = jnp.dot(work_feat[:, :channels], charge_weight, preferred_element_type=jnp.float32)
     wavevectors, weights = wave_vectors(wave_index, domains_x, domains_y)
     part_real, part_imag = structure_terms(absolute, charges, wavevectors)
-    total_real, total_imag = lax.psum((part_real, part_imag), ("gx", "yz"))
+    total_real, total_imag = treat_cells((part_real, part_imag))
     table_up = project_pair(table_feat, up_weight).astype(jnp.bfloat16)
     onehot = (
         work_species[:, None] == jnp.arange(prod_weight.shape[0], dtype=jnp.float32)[None, :]

time: 384 us -> 275 us (0.72)
  waiting for transfers between devices: 132 us -> 60.9 us
  matrix products: 152 us -> 131 us
  local copies, waits for them, and re-layouts: 29 us -> 15.1 us
    psum x1 -> x2, waiting for transfers between devices: 122 us -> 48.9 us  [review_strips_all(): block_in = jax.lax.psum(block_in, h)]
    dot_general x8, matrix products: 24.7 us -> 19.2 us  [accumulate(): return running + jnp.dot(jnp.sin(phases), sin_right, precision=highest)]
    dot_general x8, matrix products: 24.5 us -> 19.1 us  [accumulate(): running = running + jnp.dot(jnp.cos(phases), cos_right, precision=highest)]
    dot_general x4, matrix products: 18.3 us -> 13.3 us  [edge_products(): jnp.dot(hidden, radial_out, preferred_element_type=jnp.float32)]
    slice x16, local copies, waits for them, and re-layouts: 4.75 us -> 0.07 us  [phase_of(): absolute[0][:, None] * wavevectors[0][None, :]]
  transfers between devices with their start and end apart: 12 -> 13, of which waited for: 3 -> 6; matrix products, arithmetic and copies ran while one was open for 31% -> 43% of each run, Pallas kernels for 0% -> 0%
where the time goes in v1:
time: 275 us; the launch traced here: 274 us
  matrix products  131 us (48%)
  waiting for transfers between devices  60.9 us (22%)
  starting transfers between devices  25.7 us (9%)
  other arithmetic  20.2 us (7%)
  local copies, waits for them, and re-layouts  15.1 us (5%)
  between operations  14.7 us (5%)
  loops' own time  6.33 us (2%)
    psum x2, waiting for transfers between devices, review_strips_all(): block_in = jax.lax.psum(block_in, h)  48.9 us
    dot_general x8, matrix products, one_block(): jnp.einsum('ak,aq->kq', jnp.sin(phases), charges, precision=highest)  23.1 us
    dot_general x8, matrix products, one_block(): jnp.einsum('ak,aq->kq', jnp.cos(phases), charges, precision=highest)  22.9 us
    dot_general x8, matrix products, accumulate(): return running + jnp.dot(jnp.sin(phases), sin_right, precision=highest)  19.2 us
    dot_general x8, matrix products, accumulate(): running = running + jnp.dot(jnp.cos(phases), cos_right, precision=highest)  19.1 us
    reduce_sum x4, other arithmetic, neighbour_sum(): jnp.sum(values.reshape(atom_count, slot_count, channels), axis=1)  13.5 us
    dot_general x4, matrix products, edge_products(): jnp.dot(hidden, radial_out, preferred_element_type=jnp.float32)  13.3 us
    dot_general x4, matrix products, edge_products(): jnp.dot(row_onehot.astype(jnp.float32), table_pos.T, precision=highest)  12.4 us
  transfers between devices with their start and end apart: 13, of which 6 were waited for; matrix products, arithmetic and copies ran while one was open for 43% of the time, Pallas kernels for 0%

profile of v1, /device:TPU:0, one launch (start us, length us, event | category | flops | bytes accessed | tf_op | source)
XLA Modules:
  0.0 274.0 jit_solution(7925408371000439181)
XLA Ops:
  12.4 5.2 %all-to-all-start = ((bf16[8,8,128]{2,1,0:T(8,128)(2,1)}), bf16[8,8,128]{2,1,0:T(8,128)(2,1)S(1)}, u32[]{:S(2)}, u32[]{:S(2)}) async-start(bf16[8,8,128]{2,1,0:T(8,128)(2,1)} %copy.64), calls=%async_computation | async-start | bytes 32768 | tf_op jit(solution)/shard_map/all_to_all | solution.py:303
  22.3 4.0 %all-to-all-start.1 = ((bf16[8,128,512]{2,1,0:T(8,128)(2,1)}), bf16[8,128,512]{2,1,0:T(8,128)(2,1)S(1)}, u32[]{:S(2)}, u32[]{:S(2)}) async-start(bf16[8,128,512]{2,1,0:T(8,128)(2,1)} %copy.71), calls=%async_computation.1 | async-start | bytes 2097152 | tf_op jit(solution)/shard_map/all_to_all | solution.py:304
  35.1 6.1 %collective-permute-done.2 = bf16[3,1,3,32]{3,2,1,0:T(4,128)(2,1)S(1)} collective-permute-done((bf16[3,1,3,32]{3,2,1,0:T(4,128)(2,1)S(1)}, bf16[3,1,3,32]{3,2,1,0:T(4,128)(2,1)S(1)}, u32[]{:S(2)}, u32[]{:S(2)}) %collective-permute-start.2) | collective-permute-done | bytes 608 | tf_op jit(solution)/shard_map/ppermute | solution.py:34
  46.8 56.6 %while.37 = (s32[]{:T(128)}, f32[8,512,8]{1,2,0:T(8,128)}, f32[8,512,8]{1,2,0:T(8,128)}, f32[3,256]{1,0:T(4,128)S(1)}, s32[8]{0:T(128)S(1)}, /*index=5*/f32[3,40...) while((s32[]{:T(128)}, f32[8,512,8]{1,2,0:T(8,128)}, ...), condition=%wide.region_9.10_spmd, body=%wide.region_8.9_spmd.sunk | while | flops 26476552 | bytes 87259 | solution.py:68
  48.2 2.9 %fusion.239 = f32[8,512,8]{1,2,0:T(8,128)} fusion(f32[8,512,8]{1,2,0:T(8,128)} %get-tuple-element.608, s32[]{:T(128)} %get-tuple-element.606, f32[256,8]{0,1:T(8,128)S(1)} %get-tuple-element.625, f32[512]{0:T(512)S(1)} %bitcast.308, f32[256]{0:T(256)S(1)} %bitcast.319, f32[512]{0:T(512)S(1)} %bitcast.306, f32[256]{0:T(256)S(1)} %bitcast.321, ...), kind=kOutput, calls=%fused_computation.74.clone.1 | convolution fusion | flops 13238272 | bytes 34304 | tf_op jit(solution)/shard_map/while/body/eval_jaxpr/ak,aq->kq/dot_general | solution.py:65
  55.2 2.9 %fusion.239 = f32[8,512,8]{1,2,0:T(8,128)} fusion(f32[8,512,8]{1,2,0:T(8,128)} %get-tuple-element.608, s32[]{:T(128)} %get-tuple-element.606, f32[256,8]{0,1:T(8,128)S(1)} %get-tuple-element.625, f32[512]{0:T(512)S(1)} %bitcast.308, f32[256]{0:T(256)S(1)} %bitcast.319, f32[512]{0:T(512)S(1)} %bitcast.306, f32[256]{0:T(256)S(1)} %bitcast.321, ...), kind=kOutput, calls=%fused_computation.74.clone.1 | convolution fusion | flops 13238272 | bytes 34304 | tf_op jit(solution)/shard_map/while/body/eval_jaxpr/ak,aq->kq/dot_general | solution.py:65
  58.1 2.9 %fusion.238 = f32[8,512,8]{1,2,0:T(8,128)} fusion(f32[8,512,8]{1,2,0:T(8,128)} %get-tuple-element.607, s32[]{:T(128)} %get-tuple-element.606, f32[256,8]{0,1:T(8,128)S(1)} %get-tuple-element.625, f32[512]{0:T(512)S(1)} %bitcast.309, f32[256]{0:T(256)S(1)} %bitcast.320, f32[512]{0:T(512)S(1)} %bitcast.307, f32[256]{0:T(256)S(1)} %bitcast.322, ...), kind=kOutput, calls=%fused_computation.76.clone.1 | convolution fusion | flops 13238272 | bytes 34304 | tf_op jit(solution)/shard_map/while/body/eval_jaxpr/ak,aq->kq/dot_general | solution.py:64
  62.3 2.9 %fusion.239 = f32[8,512,8]{1,2,0:T(8,128)} fusion(f32[8,512,8]{1,2,0:T(8,128)} %get-tuple-element.608, s32[]{:T(128)} %get-tuple-element.606, f32[256,8]{0,1:T(8,128)S(1)} %get-tuple-element.625, f32[512]{0:T(512)S(1)} %bitcast.308, f32[256]{0:T(256)S(1)} %bitcast.319, f32[512]{0:T(512)S(1)} %bitcast.306, f32[256]{0:T(256)S(1)} %bitcast.321, ...), kind=kOutput, calls=%fused_computation.74.clone.1 | convolution fusion | flops 13238272 | bytes 34304 | tf_op jit(solution)/shard_map/while/body/eval_jaxpr/ak,aq->kq/dot_general | solution.py:65
  65.2 2.9 %fusion.238 = f32[8,512,8]{1,2,0:T(8,128)} fusion(f32[8,512,8]{1,2,0:T(8,128)} %get-tuple-element.607, s32[]{:T(128)} %get-tuple-element.606, f32[256,8]{0,1:T(8,128)S(1)} %get-tuple-element.625, f32[512]{0:T(512)S(1)} %bitcast.309, f32[256]{0:T(256)S(1)} %bitcast.320, f32[512]{0:T(512)S(1)} %bitcast.307, f32[256]{0:T(256)S(1)} %bitcast.322, ...), kind=kOutput, calls=%fused_computation.76.clone.1 | convolution fusion | flops 13238272 | bytes 34304 | tf_op jit(solution)/shard_map/while/body/eval_jaxpr/ak,aq->kq/dot_general | solution.py:64
  69.4 2.9 %fusion.239 = f32[8,512,8]{1,2,0:T(8,128)} fusion(f32[8,512,8]{1,2,0:T(8,128)} %get-tuple-element.608, s32[]{:T(128)} %get-tuple-element.606, f32[256,8]{0,1:T(8,128)S(1)} %get-tuple-element.625, f32[512]{0:T(512)S(1)} %bitcast.308, f32[256]{0:T(256)S(1)} %bitcast.319, f32[512]{0:T(512)S(1)} %bitcast.306, f32[256]{0:T(256)S(1)} %bitcast.321, ...), kind=kOutput, calls=%fused_computation.74.clone.1 | convolution fusion | flops 13238272 | bytes 34304 | tf_op jit(solution)/shard_map/while/body/eval_jaxpr/ak,aq->kq/dot_general | solution.py:65
  76.5 2.9 %fusion.239 = f32[8,512,8]{1,2,0:T(8,128)} fusion(f32[8,512,8]{1,2,0:T(8,128)} %get-tuple-element.608, s32[]{:T(128)} %get-tuple-element.606, f32[256,8]{0,1:T(8,128)S(1)} %get-tuple-element.625, f32[512]{0:T(512)S(1)} %bitcast.308, f32[256]{0:T(256)S(1)} %bitcast.319, f32[512]{0:T(512)S(1)} %bitcast.306, f32[256]{0:T(256)S(1)} %bitcast.321, ...), kind=kOutput, calls=%fused_computation.74.clone.1 | convolution fusion | flops 13238272 | bytes 34304 | tf_op jit(solution)/shard_map/while/body/eval_jaxpr/ak,aq->kq/dot_general | solution.py:65
  83.6 2.9 %fusion.239 = f32[8,512,8]{1,2,0:T(8,128)} fusion(f32[8,512,8]{1,2,0:T(8,128)} %get-tuple-element.608, s32[]{:T(128)} %get-tuple-element.606, f32[256,8]{0,1:T(8,128)S(1)} %get-tuple-element.625, f32[512]{0:T(512)S(1)} %bitcast.308, f32[256]{0:T(256)S(1)} %bitcast.319, f32[512]{0:T(512)S(1)} %bitcast.306, f32[256]{0:T(256)S(1)} %bitcast.321, ...), kind=kOutput, calls=%fused_computation.74.clone.1 | convolution fusion | flops 13238272 | bytes 34304 | tf_op jit(solution)/shard_map/while/body/eval_jaxpr/ak,aq->kq/dot_general | solution.py:65
  90.6 2.9 %fusion.239 = f32[8,512,8]{1,2,0:T(8,128)} fusion(f32[8,512,8]{1,2,0:T(8,128)} %get-tuple-element.608, s32[]{:T(128)} %get-tuple-element.606, f32[256,8]{0,1:T(8,128)S(1)} %get-tuple-element.625, f32[512]{0:T(512)S(1)} %bitcast.308, f32[256]{0:T(256)S(1)} %bitcast.319, f32[512]{0:T(512)S(1)} %bitcast.306, f32[256]{0:T(256)S(1)} %bitcast.321, ...), kind=kOutput, calls=%fused_computation.74.clone.1 | convolution fusion | flops 13238272 | bytes 34304 | tf_op jit(solution)/shard_map/while/body/eval_jaxpr/ak,aq->kq/dot_general | solution.py:65
  97.7 2.9 %fusion.239 = f32[8,512,8]{1,2,0:T(8,128)} fusion(f32[8,512,8]{1,2,0:T(8,128)} %get-tuple-element.608, s32[]{:T(128)} %get-tuple-element.606, f32[256,8]{0,1:T(8,128)S(1)} %get-tuple-element.625, f32[512]{0:T(512)S(1)} %bitcast.308, f32[256]{0:T(256)S(1)} %bitcast.319, f32[512]{0:T(512)S(1)} %bitcast.306, f32[256]{0:T(256)S(1)} %bitcast.321, ...), kind=kOutput, calls=%fused_computation.74.clone.1 | convolution fusion | flops 13238272 | bytes 34304 | tf_op jit(solution)/shard_map/while/body/eval_jaxpr/ak,aq->kq/dot_general | solution.py:65
  100.6 2.9 %fusion.238 = f32[8,512,8]{1,2,0:T(8,128)} fusion(f32[8,512,8]{1,2,0:T(8,128)} %get-tuple-element.607, s32[]{:T(128)} %get-tuple-element.606, f32[256,8]{0,1:T(8,128)S(1)} %get-tuple-element.625, f32[512]{0:T(512)S(1)} %bitcast.309, f32[256]{0:T(256)S(1)} %bitcast.320, f32[512]{0:T(512)S(1)} %bitcast.307, f32[256]{0:T(256)S(1)} %bitcast.322, ...), kind=kOutput, calls=%fused_computation.76.clone.1 | convolution fusion | flops 13238272 | bytes 34304 | tf_op jit(solution)/shard_map/while/body/eval_jaxpr/ak,aq->kq/dot_general | solution.py:64
  106.9 48.9 %all-reduce.5.cloned.1.call-done = (f32[4096,8]{0,1:T(8,128)}, f32[4096,8]{0,1:T(8,128)}) async-done(((f32[4096,8]{0,1:T(8,128)}, f32[4096,8]{0,1:T(8,128)}), (f32[4096,8]{0,1:T(8,128)}, f32[4096,8]{0,1:T(8,128)})) %all-reduce.5.cloned.1.call-update) | async-done | bytes 262160 | tf_op jit(solution)/shard_map/psum | solution.py:20
  156.9 57.3 %while.36 = (s32[]{:T(128)}, bf16[4,64,512]{2,1,0:T(8,128)(2,1)S(1)}, f32[4,64,640]{2,1,0:T(8,128)S(1)}, s32[4,64,64]{2,1,0:T(8,128)S(1)}, f32[3,384]{1,0:T(4,12...) while((s32[]{:T(128)}, ...), condition=%wide.region_6.7_spmd, body=%wide.region_0.6_spmd.sunk | while | flops 2032549888 | bytes 45476804 | solution.py:369
  157.4 3.1 %multiply_reduce_fusion.7 = (f32[4096]{0:T(1024)S(1)}, f32[3,4096]{1,0:T(4,128)S(1)}) fusion(f32[3,4096]{1,0:T(4,128)S(1)} %sub.133, f32[3,384]{1,0:T(4,128)S(1)} %get-tuple-element.585, s32[4096]{0:T(1024)S(1)} %eq.279), kind=kOutput, calls=%fused_computation.31.clone.1 | convolution fusion | flops 58228736 | bytes 135680 | tf_op jit(solution)/shard_map/while/body/eval_jaxpr/dot_general | solution.py:121
  161.6 3.3 %multiply_convert_fusion.13 = bf16[4096,512]{1,0:T(8,128)(2,1)} fusion(bf16[64,512]{1,0:T(8,128)(2,1)S(1)} %get-tuple-element.589, f32[4096]{0:T(1024)S(1)} %get-tuple-element.519, bf16[4096,64]{0,1:T(8,128)(2,1)S(1)} %multiply_convert_fusion.12, bf16[2,64,64]{2,1,0:T(8,128)(2,1)S(1)} %get-tuple-element.588), kind=kOutput, calls=%fused_computation.clone.1 | convolution fusion | flops 307494912 | bytes 4816896 | tf_op jit(solution)/shard_map/while/body/eval_jaxpr/dot_general | solution.py:148
  167.9 3.4 %bitcast_reduce_fusion.5 = (f32[64,128]{1,0:T(8,128)S(1)}, f32[64,128]{1,0:T(8,128)S(1)}, f32[64,128]{1,0:T(8,128)S(1)}, f32[64,128]{1,0:T(8,128)S(1)}) fusion(f32[4096,512]{1,0:T(8,128)S(1)} %fusion.227, f32[4096]{0:T(1024)S(1)} %mul.1019, bf16[4096,512]{1,0:T(8,128)(2,1)S(1)} %copy-done.1, f32[4096]{0:T(1024)S(1)} %mul.1020, f32[4096]{0:T(1024)S(1)} %mul.1021), kind=kLoop, calls=%fused_computation.15.clone.1 | loop fusion | flops 13598720 | bytes 12763136 | tf_op jit(solution)/shard_map/while/body/eval_jaxpr/reduce_sum | solution.py:160
  171.7 3.1 %multiply_reduce_fusion.7 = (f32[4096]{0:T(1024)S(1)}, f32[3,4096]{1,0:T(4,128)S(1)}) fusion(f32[3,4096]{1,0:T(4,128)S(1)} %sub.133, f32[3,384]{1,0:T(4,128)S(1)} %get-tuple-element.585, s32[4096]{0:T(1024)S(1)} %eq.279), kind=kOutput, calls=%fused_computation.31.clone.1 | convolution fusion | flops 58228736 | bytes 135680 | tf_op jit(solution)/shard_map/while/body/eval_jaxpr/dot_general | solution.py:121
  175.9 3.3 %multiply_convert_fusion.13 = bf16[4096,512]{1,0:T(8,128)(2,1)} fusion(bf16[64,512]{1,0:T(8,128)(2,1)S(1)} %get-tuple-element.589, f32[4096]{0:T(1024)S(1)} %get-tuple-element.519, bf16[4096,64]{0,1:T(8,128)(2,1)S(1)} %multiply_convert_fusion.12, bf16[2,64,64]{2,1,0:T(8,128)(2,1)S(1)} %get-tuple-element.588), kind=kOutput, calls=%fused_computation.clone.1 | convolution fusion | flops 307494912 | bytes 4816896 | tf_op jit(solution)/shard_map/while/body/eval_jaxpr/dot_general | solution.py:148
  182.2 3.4 %bitcast_reduce_fusion.5 = (f32[64,128]{1,0:T(8,128)S(1)}, f32[64,128]{1,0:T(8,128)S(1)}, f32[64,128]{1,0:T(8,128)S(1)}, f32[64,128]{1,0:T(8,128)S(1)}) fusion(f32[4096,512]{1,0:T(8,128)S(1)} %fusion.227, f32[4096]{0:T(1024)S(1)} %mul.1019, bf16[4096,512]{1,0:T(8,128)(2,1)S(1)} %copy-done.1, f32[4096]{0:T(1024)S(1)} %mul.1020, f32[4096]{0:T(1024)S(1)} %mul.1021), kind=kLoop, calls=%fused_computation.15.clone.1 | loop fusion | flops 13598720 | bytes 12763136 | tf_op jit(solution)/shard_map/while/body/eval_jaxpr/reduce_sum | solution.py:160
  186.0 3.1 %multiply_reduce_fusion.7 = (f32[4096]{0:T(1024)S(1)}, f32[3,4096]{1,0:T(4,128)S(1)}) fusion(f32[3,4096]{1,0:T(4,128)S(1)} %sub.133, f32[3,384]{1,0:T(4,128)S(1)} %get-tuple-element.585, s32[4096]{0:T(1024)S(1)} %eq.279), kind=kOutput, calls=%fused_computation.31.clone.1 | convolution fusion | flops 58228736 | bytes 135680 | tf_op jit(solution)/shard_map/while/body/eval_jaxpr/dot_general | solution.py:121
  190.2 3.3 %multiply_convert_fusion.13 = bf16[4096,512]{1,0:T(8,128)(2,1)} fusion(bf16[64,512]{1,0:T(8,128)(2,1)S(1)} %get-tuple-element.589, f32[4096]{0:T(1024)S(1)} %get-tuple-element.519, bf16[4096,64]{0,1:T(8,128)(2,1)S(1)} %multiply_convert_fusion.12, bf16[2,64,64]{2,1,0:T(8,128)(2,1)S(1)} %get-tuple-element.588), kind=kOutput, calls=%fused_computation.clone.1 | convolution fusion | flops 307494912 | bytes 4816896 | tf_op jit(solution)/shard_map/while/body/eval_jaxpr/dot_general | solution.py:148
  196.5 3.4 %bitcast_reduce_fusion.5 = (f32[64,128]{1,0:T(8,128)S(1)}, f32[64,128]{1,0:T(8,128)S(1)}, f32[64,128]{1,0:T(8,128)S(1)}, f32[64,128]{1,0:T(8,128)S(1)}) fusion(f32[4096,512]{1,0:T(8,128)S(1)} %fusion.227, f32[4096]{0:T(1024)S(1)} %mul.1019, bf16[4096,512]{1,0:T(8,128)(2,1)S(1)} %copy-done.1, f32[4096]{0:T(1024)S(1)} %mul.1020, f32[4096]{0:T(1024)S(1)} %mul.1021), kind=kLoop, calls=%fused_computation.15.clone.1 | loop fusion | flops 13598720 | bytes 12763136 | tf_op jit(solution)/shard_map/while/body/eval_jaxpr/reduce_sum | solution.py:160
  200.3 3.1 %multiply_reduce_fusion.7 = (f32[4096]{0:T(1024)S(1)}, f32[3,4096]{1,0:T(4,128)S(1)}) fusion(f32[3,4096]{1,0:T(4,128)S(1)} %sub.133, f32[3,384]{1,0:T(4,128)S(1)} %get-tuple-element.585, s32[4096]{0:T(1024)S(1)} %eq.279), kind=kOutput, calls=%fused_computation.31.clone.1 | convolution fusion | flops 58228736 | bytes 135680 | tf_op jit(solution)/shard_map/while/body/eval_jaxpr/dot_general | solution.py:121
  204.5 3.3 %multiply_convert_fusion.13 = bf16[4096,512]{1,0:T(8,128)(2,1)} fusion(bf16[64,512]{1,0:T(8,128)(2,1)S(1)} %get-tuple-element.589, f32[4096]{0:T(1024)S(1)} %get-tuple-element.519, bf16[4096,64]{0,1:T(8,128)(2,1)S(1)} %multiply_convert_fusion.12, bf16[2,64,64]{2,1,0:T(8,128)(2,1)S(1)} %get-tuple-element.588), kind=kOutput, calls=%fused_computation.clone.1 | convolution fusion | flops 307494912 | bytes 4816896 | tf_op jit(solution)/shard_map/while/body/eval_jaxpr/dot_general | solution.py:148
  210.8 3.4 %bitcast_reduce_fusion.5 = (f32[64,128]{1,0:T(8,128)S(1)}, f32[64,128]{1,0:T(8,128)S(1)}, f32[64,128]{1,0:T(8,128)S(1)}, f32[64,128]{1,0:T(8,128)S(1)}) fusion(f32[4096,512]{1,0:T(8,128)S(1)} %fusion.227, f32[4096]{0:T(1024)S(1)} %mul.1019, bf16[4096,512]{1,0:T(8,128)(2,1)S(1)} %copy-done.1, f32[4096]{0:T(1024)S(1)} %mul.1020, f32[4096]{0:T(1024)S(1)} %mul.1021), kind=kLoop, calls=%fused_computation.15.clone.1 | loop fusion | flops 13598720 | bytes 12763136 | tf_op jit(solution)/shard_map/while/body/eval_jaxpr/reduce_sum | solution.py:160
  216.9 39.2 %while.38 = (s32[]{:T(128)}, f32[256,32]{0,1:T(8,128)S(1)}, f32[3,256]{1,0:T(4,128)S(1)}, f32[3,4096]{1,0:T(4,128)S(1)}, f32[4096,32]{0,1:T(8,128)S(1)}, /*index...) while((s32[]{:T(128)}, f32[256,32]{0,1:T(8,128)S(1)}, ...), condition=%wide.region_15.16_spmd.clone, body=%wide.region_14.15_spmd.clone.sunk | while | flops 101998600 | bytes 299225 | solution.py:96
  257.8 3.3 %all-to-all-start.2 = ((f32[8,4,128]{2,1,0:T(4,128)}), f32[8,4,128]{2,1,0:T(4,128)S(1)}, u32[]{:S(2)}, u32[]{:S(2)}) async-start(f32[8,4,128]{2,1,0:T(4,128)} %copy.79), calls=%async_computation.2 | async-start | bytes 32768 | tf_op jit(solution)/shard_map/all_to_all | solution.py:396
  261.3 4.5 %all-to-all-done.2 = f32[8,4,128]{2,1,0:T(4,128)S(1)} async-done(((f32[8,4,128]{2,1,0:T(4,128)}), f32[8,4,128]{2,1,0:T(4,128)S(1)}, u32[]{:S(2)}, u32[]{:S(2)}) %all-to-all-start.2) | async-done | bytes 16416 | tf_op jit(solution)/shard_map/all_to_all | solution.py:396
  (319 shorter events, 110.0 us)
Async XLA Ops:
  7.2 11.3 %copy-start = (bf16[256,512]{1,0:T(8,128)(2,1)S(1)}, bf16[256,512]{1,0:T(8,128)(2,1)}, u32[]{:S(2)}) copy-start(bf16[256,512]{1,0:T(8,128)(2,1)} %param.30) | copy-start | bytes 786436
  7.2 13.1 %copy-start.14 = (f32[3]{0:T(128)S(1)}, f32[3]{0:T(128)}, u32[]{:S(2)}) copy-start(f32[3]{0:T(128)} %constant.114.clone) | copy-start | bytes 40
  7.2 13.1 %copy-start.6 = (s32[3,4096]{1,0:T(4,128)S(1)}, s32[3,4096]{1,0:T(4,128)}, u32[]{:S(2)}) copy-start(s32[3,4096]{1,0:T(4,128)} %param.36) | copy-start | bytes 147460
  12.4 10.0 %all-to-all-start = ((bf16[8,8,128]{2,1,0:T(8,128)(2,1)}), bf16[8,8,128]{2,1,0:T(8,128)(2,1)S(1)}, u32[]{:S(2)}, u32[]{:S(2)}) async-start(bf16[8,8,128]{2,1,0:T(8,128)(2,1)} %copy.64), calls=%async_computation | async-start | bytes 32768 | tf_op jit(solution)/shard_map/all_to_all | solution.py:303
  18.5 3.4 %copy-start.2 = (s32[256,64]{0,1:T(8,128)S(1)}, s32[256,64]{0,1:T(8,128)}, u32[]{:S(2)}) copy-start(s32[256,64]{0,1:T(8,128)} %param.34) | copy-start | bytes 196612
  20.6 6.1 %copy-start.13 = (s32[32]{0:T(128)S(1)}, s32[32]{0:T(128)}, u32[]{:S(2)}) copy-start(s32[32]{0:T(128)} %param.33) | copy-start | bytes 388
  20.6 10.4 %copy-start.7 = (f32[6,640]{1,0:T(8,128)S(1)}, f32[6,640]{1,0:T(8,128)}, u32[]{:S(2)}) copy-start(f32[6,640]{1,0:T(8,128)} %param.41) | copy-start | bytes 46084
  22.3 19.4 %all-to-all-start.1 = ((bf16[8,128,512]{2,1,0:T(8,128)(2,1)}), bf16[8,128,512]{2,1,0:T(8,128)(2,1)S(1)}, u32[]{:S(2)}, u32[]{:S(2)}) async-start(bf16[8,128,512]{2,1,0:T(8,128)(2,1)} %copy.71), calls=%async_computation.1 | async-start | bytes 2097152 | tf_op jit(solution)/shard_map/all_to_all | solution.py:304
  26.4 20.3 %copy-start.17 = (bf16[128,8]{0,1:T(8,128)(2,1)S(1)}, bf16[128,8]{0,1:T(8,128)(2,1)}, u32[]{:S(2)}) copy-start(bf16[128,8]{0,1:T(8,128)(2,1)} %param.44) | copy-start | bytes 6148
  26.4 129.5 %all-reduce.5.cloned.1.call-start = ((), (), s32[]{:S(2)}) async-start(), calls=%async_computation.3 | async-start | bytes 524288 | tf_op jit(solution)/shard_map/psum | solution.py:20
  26.9 5.4 %collective-permute-start = (bf16[1,1,3,32]{3,2,1,0:T(4,128)(2,1)S(1)}, bf16[1,1,3,32]{3,2,1,0:T(4,128)(2,1)S(1)}, u32[]{:S(2)}, u32[]{:S(2)}) collective-permute-start(bf16[1,1,3,32]{3,2,1,0:T(4,128)(2,1)S(1)} %fusion.86), channel_id=1, source_target_pairs={{0,8},{8,16},{16,24},{24,0},{1,9},{9,17},{17,25},{25,1},{2,10},{10... | collective-permute-start | bytes 584 | tf_op jit(solution)/shard_map/ppermute | solution.py:34
  28.5 3.8 %collective-permute-start.1 = (bf16[1,1,3,32]{3,2,1,0:T(4,128)(2,1)S(1)}, bf16[1,1,3,32]{3,2,1,0:T(4,128)(2,1)S(1)}, u32[]{:S(2)}, u32[]{:S(2)}) collective-permute-start(bf16[1,1,3,32]{3,2,1,0:T(4,128)(2,1)S(1)} %fusion.86), channel_id=1, source_target_pairs={{8,0},{16,8},{24,16},{0,24},{9,1},{17,9},{25,17},{1,25},{10,2},{18... | collective-permute-start | bytes 584 | tf_op jit(solution)/shard_map/ppermute | solution.py:35
  32.3 8.9 %collective-permute-start.2 = (bf16[3,1,3,32]{3,2,1,0:T(4,128)(2,1)S(1)}, bf16[3,1,3,32]{3,2,1,0:T(4,128)(2,1)S(1)}, u32[]{:S(2)}, u32[]{:S(2)}) collective-permute-start(bf16[3,1,3,32]{3,2,1,0:T(4,128)(2,1)S(1)} %pad_maximum_fusion.5), channel_id=1, source_target_pairs={{0,1},{1,2},{2,3},{3,4},{4,5},{5,6},{6,7},{7,0},{8,9},{9,10},{10,1... | collective-permute-start | bytes 1736 | tf_op jit(solution)/shard_map/ppermute | solution.py:34
  32.4 8.8 %collective-permute-start.3 = (bf16[3,1,3,32]{3,2,1,0:T(4,128)(2,1)S(1)}, bf16[3,1,3,32]{3,2,1,0:T(4,128)(2,1)S(1)}, u32[]{:S(2)}, u32[]{:S(2)}) collective-permute-start(bf16[3,1,3,32]{3,2,1,0:T(4,128)(2,1)S(1)} %pad_maximum_fusion.5), channel_id=1, source_target_pairs={{1,0},{2,1},{3,2},{4,3},{5,4},{6,5},{7,6},{0,7},{9,8},{10,9},{11,1... | collective-permute-start | bytes 1736 | tf_op jit(solution)/shard_map/ppermute | solution.py:35
  42.8 61.3 %collective-permute-start.4 = (bf16[1,1,32,512]{3,2,1,0:T(8,128)(2,1)S(1)}, bf16[1,1,32,512]{3,2,1,0:T(8,128)(2,1)S(1)}, u32[]{:S(2)}, u32[]{:S(2)}) collective-permute-start(bf16[1,1,32,512]{3,2,1,0:T(8,128)(2,1)S(1)} %fusion.84), channel_id=1, source_target_pairs={{0,8},{8,16},{16,24},{24,0},{1,9},{9,17},{17,25},{25,1},{2,10},{10... | collective-permute-start | bytes 98312 | tf_op jit(solution)/shard_map/ppermute | solution.py:34
  44.4 59.7 %collective-permute-start.5 = (bf16[1,1,32,512]{3,2,1,0:T(8,128)(2,1)S(1)}, bf16[1,1,32,512]{3,2,1,0:T(8,128)(2,1)S(1)}, u32[]{:S(2)}, u32[]{:S(2)}) collective-permute-start(bf16[1,1,32,512]{3,2,1,0:T(8,128)(2,1)S(1)} %fusion.84), channel_id=1, source_target_pairs={{8,0},{16,8},{24,16},{0,24},{9,1},{17,9},{25,17},{1,25},{10,2},{18... | collective-permute-start | bytes 98312 | tf_op jit(solution)/shard_map/ppermute | solution.py:35
  46.8 56.7 %copy-start.3 = (bf16[2,128,128]{2,1,0:T(8,128)(2,1)S(1)}, bf16[2,128,128]{2,1,0:T(8,128)(2,1)}, u32[]{:S(2)}) copy-start(bf16[2,128,128]{2,1,0:T(8,128)(2,1)} %param.43) | copy-start | bytes 196612
  103.7 52.4 %copy-start.4 = (bf16[2,128,128]{2,1,0:T(8,128)(2,1)S(1)}, bf16[2,128,128]{2,1,0:T(8,128)(2,1)}, u32[]{:S(2)}) copy-start(bf16[2,128,128]{2,1,0:T(8,128)(2,1)} %param.40) | copy-start | bytes 196612
  104.1 111.5 %all-reduce.7.cloned.1.call-start = ((), (), s32[]{:S(2)}) async-start(), calls=%async_computation.4 | async-start | bytes 524288 | tf_op jit(solution)/shard_map/psum | solution.py:20
  104.2 52.7 %copy-start.15 = (bf16[64,512]{1,0:T(8,128)(2,1)S(1)}, bf16[64,512]{1,0:T(8,128)(2,1)}, u32[]{:S(2)}) copy-start(bf16[64,512]{1,0:T(8,128)(2,1)} %param.39) | copy-start | bytes 196612
  104.2 52.7 %copy-start.16 = (bf16[2,64,64]{2,1,0:T(8,128)(2,1)S(1)}, bf16[2,64,64]{2,1,0:T(8,128)(2,1)}, u32[]{:S(2)}) copy-start(bf16[2,64,64]{2,1,0:T(8,128)(2,1)} %param.38) | copy-start | bytes 49156
  104.2 52.7 %copy-start.18 = (bf16[8,64]{1,0:T(8,128)(2,1)S(1)}, bf16[8,64]{1,0:T(8,128)(2,1)}, u32[]{:S(2)}) copy-start(bf16[8,64]{1,0:T(8,128)(2,1)} %param.37) | copy-start | bytes 3076
  104.2 51.7 %collective-permute-start.6 = (bf16[3,1,32,512]{3,2,1,0:T(8,128)(2,1)S(1)}, bf16[3,1,32,512]{3,2,1,0:T(8,128)(2,1)S(1)}, u32[]{:S(2)}, u32[]{:S(2)}) collective-permute-start(bf16[3,1,32,512]{3,2,1,0:T(8,128)(2,1)S(1)} %pad_maximum_fusion.3), channel_id=1, source_target_pairs={{0,1},{1,2},{2,3},{3,4},{4,5},{5,6},{6,7},{7,0},{8,9},{9,10},{10,1... | collective-permute-start | bytes 294920 | tf_op jit(solution)/shard_map/ppermute | solution.py:34
  104.3 51.6 %collective-permute-start.7 = (bf16[3,1,32,512]{3,2,1,0:T(8,128)(2,1)S(1)}, bf16[3,1,32,512]{3,2,1,0:T(8,128)(2,1)S(1)}, u32[]{:S(2)}, u32[]{:S(2)}) collective-permute-start(bf16[3,1,32,512]{3,2,1,0:T(8,128)(2,1)S(1)} %pad_maximum_fusion.3), channel_id=1, source_target_pairs={{1,0},{2,1},{3,2},{4,3},{5,4},{6,5},{7,6},{0,7},{9,8},{10,9},{11,1... | collective-permute-start | bytes 294920 | tf_op jit(solution)/shard_map/ppermute | solution.py:35
  156.9 57.5 %copy-start.5 = (bf16[2,128,128]{2,1,0:T(8,128)(2,1)S(1)}, bf16[2,128,128]{2,1,0:T(8,128)(2,1)}, u32[]{:S(2)}) copy-start(bf16[2,128,128]{2,1,0:T(8,128)(2,1)} %param.42) | copy-start | bytes 196612
  165.4 2.5 copy-start.1
  216.8 39.3 %copy-start.9 = (f32[8,128]{1,0:T(8,128)S(1)}, f32[8,128]{1,0:T(8,128)}, u32[]{:S(2)}) copy-start(f32[8,128]{1,0:T(8,128)} %param.45) | copy-start | bytes 12292
  216.8 39.8 %copy-start.10 = (bf16[128,16]{0,1:T(8,128)(2,1)S(1)}, bf16[128,16]{0,1:T(8,128)(2,1)}, u32[]{:S(2)}) copy-start(bf16[128,16]{0,1:T(8,128)(2,1)} %param.46) | copy-start | bytes 12292
  216.8 39.9 %copy-start.19 = (f32[16]{0:T(128)S(1)}, f32[16]{0:T(128)}, u32[]{:S(2)}) copy-start(f32[16]{0:T(128)} %param.47) | copy-start | bytes 196
  216.8 44.3 %copy-start.20 = (s32[2]{0:T(128)S(1)}, s32[2]{0:T(128)}, u32[]{:S(2)}) copy-start(s32[2]{0:T(128)} %param.32) | copy-start | bytes 28
  216.8 49.0 %copy-start.11 = (s32[2]{0:T(128)S(1)}, s32[2]{0:T(128)}, u32[]{:S(2)}) copy-start(s32[2]{0:T(128)} %param.31) | copy-start | bytes 28
  257.8 8.0 %all-to-all-start.2 = ((f32[8,4,128]{2,1,0:T(4,128)}), f32[8,4,128]{2,1,0:T(4,128)S(1)}, u32[]{:S(2)}, u32[]{:S(2)}) async-start(f32[8,4,128]{2,1,0:T(4,128)} %copy.79), calls=%async_computation.2 | async-start | bytes 32768 | tf_op jit(solution)/shard_map/all_to_all | solution.py:396
  (5 other events, 10.4 us)
Sparse Core Ops, SparseCore 0:
  104.2 51.6 all-reduce.4
  158.2 35.0 all-reduce.6
